TPU v7x, 512 devices: a whole 4x4x16 slice. The times are simulated.
512 devices in a mesh: swath: 32 (over z, core), chan: 16 (over x, y).
Axes of the slice: x: 4, y: 4, z: 16, core: 2. Of those that a mesh axis runs over, the one named last changes fastest.
Arguments:
- grid_profiles: bfloat16 [32768, 256], P('swath'), may hold values from -6 to 6
- send_lists: int32 [32, 32, 128], P('swath'), may hold values from 0 to 1023
- counts: int32 [32, 32], P('swath'), may hold values from 1 to 128, as said below
- angle_index: int32 [128], replicated, may hold values from 0 to 7
- jacobian: bfloat16 [3, 256, 608], P(None, None, 'chan'), may hold values from -0.375 to 0.375
- observed: bfloat16 [608, 131072], P('chan', 'swath'), may hold values from -6 to 6
- kappa: float32 [2, 608], P(None, 'chan'), may hold values from 0.04 to 0.24
- factor: bfloat16 [608, 608], P('chan')
Outputs:
- weighted: float32 [608, 131072], P('chan', 'swath')
Inputs may be any that keep to these rules, and one draw needn't show every extreme that they name: `counts`: some receiver gets 128 live slots from every sender; every entry is at least one.
All inputs are finite; a program needn't handle non-finite values.
Results may differ from a plain program's by a relative error of at most 0.0029.
Values may be sent and summed in bfloat16 or wider, within the bound.
A program may use at most 64 MiB of HBM per device.

v0:
```python
import math
import jax
import jax.numpy as jnp
from jax import lax
from jax.sharding import PartitionSpec as P

XTRACK = 128
NANG = 8
max_zenith = math.pi / 3.0


def extended_2(block, sides, width):
    for axis, dim in sides:
        count = lax.axis_size(axis)
        forward = [(i, i + 1) for i in range(count - 1)]
        backward = [(target, source) for source, target in forward]
        low = lax.ppermute(
            lax.slice_in_dim(block, block.shape[dim] - width, None, axis=dim), axis, forward
        )
        high = lax.ppermute(lax.slice_in_dim(block, 0, width, axis=dim), axis, backward)
        block = jnp.concatenate([low, block, high], axis=dim)
    return block


def diffuse_once(extended, along_rate, cross_rate):
    center = extended[:, 1:-1]
    along_sum = extended[:, 2:] + extended[:, :-2] - 2.0 * center
    side_pad = jnp.pad(center, ((0, 0), (0, 0), (1, 1)))
    cross_sum = side_pad[:, :, 2:] + side_pad[:, :, :-2] - 2.0 * center
    return center + along_rate * along_sum + cross_rate * cross_sum


def line_rims(smooth_field):
    return extended_2(smooth_field, (("swath", 1),), 1)


def on_device(grid_profiles, send_lists, counts, angle_index, jacobian, observed, kappa, factor):
    slot_rows = send_lists[0]
    slots = slot_rows.shape[1]
    own_chan = observed.shape[0]
    pixel_count = observed.shape[1]
    line_count = pixel_count // XTRACK
    live_slot = jnp.arange(slots, dtype=jnp.int32)[None, :] < counts[0][:, None]
    zero_value = jnp.zeros((), grid_profiles.dtype)
    outgoing = jnp.where(live_slot[:, :, None], grid_profiles[slot_rows], zero_value)
    incoming = lax.all_to_all(outgoing, "swath", split_axis=0, concat_axis=0, tiled=True)
    pixel_profiles = incoming.reshape(pixel_count, grid_profiles.shape[1])
    model = jnp.einsum("mkc,pk->mcp", jacobian, pixel_profiles, preferred_element_type=jnp.float32)
    zenith = angle_index.astype(jnp.float32) * (max_zenith / (NANG - 1))
    slant_path = 1.0 / jnp.cos(zenith) - 1.0
    model = model.reshape(3, own_chan, line_count, XTRACK)
    departure = observed.astype(jnp.float32).reshape(own_chan, line_count, XTRACK) - (
        model[0] + slant_path * model[1] + slant_path * slant_path * model[2]
    )
    along_rate = kappa[0][:, None, None]
    cross_rate = kappa[1][:, None, None]
    smooth_field = departure
    for sweep in range(3):
        smooth_field = diffuse_once(line_rims(smooth_field), along_rate, cross_rate)
    smoothed = smooth_field.reshape(own_chan, pixel_count).astype(jnp.bfloat16)
    return jnp.dot(
        factor,
        lax.all_gather(smoothed, "chan", axis=0, tiled=True),
        preferred_element_type=jnp.float32,
    )


def solution(mesh):
    in_specs = (
        P("swath", None),
        P("swath", None, None),
        P("swath", None),
        P(),
        P(None, None, "chan"),
        P("chan", "swath"),
        P(None, "chan"),
        P("chan", None),
    )
    out_specs = P("chan", "swath")
    return jax.shard_map(
        on_device, mesh=mesh, in_specs=in_specs, out_specs=out_specs, check_vma=False
    )
```

profile of v0, /device:TPU:1, one launch (start us, length us, event | category | flops | bytes accessed | tf_op | source)
XLA Modules:
  0.0 252.0 jit_solution(1715933017502331585)
XLA Ops:
  6.5 0.0 copy-start
  6.5 0.8 iota_compare_fusion
  7.3 0.7 fusion.29
  8.0 0.0 copy-done
  8.1 14.6 %gather_fusion = bf16[4096,256]{1,0:T(8,128)(2,1)S(1)} fusion(bf16[1024,256]{1,0:T(8,128)(2,1)S(1)} %copy-done, s32[4096]{0:T(1024)S(1)} %fusion.29), kind=kCustom, calls=%fused_computation | custom fusion | bytes 4210688 | tf_op jit(solution)/shard_map/gather | solution.py:45
  22.7 1.7 broadcast_select_fusion
  24.4 0.0 copy-start.1
  24.4 16.9 %all-to-all-start = ((bf16[32,128,256]{2,1,0:T(8,128)(2,1)}), bf16[32,128,256]{2,1,0:T(8,128)(2,1)S(1)}, u32[]{:S(2)}, u32[]{:S(2)}) async-start(bf16[32,128,256]{2,1,0:T(8,128)(2,1)} %broadcast_select_fusion), calls=%async_computation | async-start | bytes 4194304 | tf_op jit(solution)/shard_map/all_to_all | solution.py:46
  41.2 0.0 copy-start.5
  41.3 0.0 copy-start.2
  41.3 0.0 all-gather.3.cloned.1.call-start
  41.3 0.0 copy-done.1
  41.4 0.1 copy.9
  41.5 0.4 copy-done.5
  42.0 97.9 %all-to-all-done = bf16[32,128,256]{2,1,0:T(8,128)(2,1)S(1)} async-done(((bf16[32,128,256]{2,1,0:T(8,128)(2,1)}), bf16[32,128,256]{2,1,0:T(8,128)(2,1)S(1)}, u32[]{:S(2)}, u32[]{:S(2)}) %all-to-all-start) | async-done | bytes 2097184 | tf_op jit(solution)/shard_map/all_to_all | solution.py:46
  139.9 0.0 copy-done.2
  139.9 0.8 convolution_bitcast_fusion
  140.7 0.2 fusion.31
  140.8 0.1 copy.10
  141.0 0.1 copy.12
  141.1 0.0 copy-start.4
  141.1 0.1 copy.11
  141.2 0.3 fusion.14
  141.6 2.8 %collective-permute-start = (f32[38,1,128]{2,1,0:T(1,128)S(1)}, f32[38,1,128]{2,1,0:T(1,128)S(1)}, u32[]{:S(2)}, u32[]{:S(2)}) collective-permute-start(f32[38,1,128]{2,1,0:T(1,128)S(1)} %get-tuple-element.14), channel_id=1, source_target_pairs={{16,0},{32,16},{48,32},{64,48},{80,64},{96,80},{112,96},{128,112},... | collective-permute-start | bytes 58376 | tf_op jit(solution)/shard_map/ppermute | solution.py:20
  144.3 4.2 %collective-permute-start.1 = (f32[38,1,128]{2,1,0:T(1,128)S(1)}, f32[38,1,128]{2,1,0:T(1,128)S(1)}, u32[]{:S(2)}, u32[]{:S(2)}) collective-permute-start(f32[38,1,128]{2,1,0:T(1,128)S(1)} %get-tuple-element.15), channel_id=1, source_target_pairs={{0,16},{16,32},{32,48},{48,64},{64,80},{80,96},{96,112},{112,128},... | collective-permute-start | bytes 58376 | tf_op jit(solution)/shard_map/ppermute | solution.py:17
  148.6 0.0 copy-done.4
  148.6 0.0 collective-permute-done
  148.6 0.8 collective-permute-done.1
  149.4 0.5 fusion.3
  150.0 1.9 collective-permute-start.2
  151.9 4.2 %collective-permute-start.3 = (f32[38,1,128]{2,1,0:T(1,128)S(1)}, f32[38,1,128]{2,1,0:T(1,128)S(1)}, u32[]{:S(2)}, u32[]{:S(2)}) collective-permute-start(f32[38,1,128]{2,1,0:T(1,128)S(1)} %get-tuple-element.13), channel_id=1, source_target_pairs={{0,16},{16,32},{32,48},{48,64},{64,80},{80,96},{96,112},{112,128},... | collective-permute-start | bytes 58376 | tf_op jit(solution)/shard_map/ppermute | solution.py:17
  156.2 0.0 collective-permute-done.2
  156.2 0.9 collective-permute-done.3
  157.0 0.5 fusion.7
  157.6 1.9 collective-permute-start.4
  159.5 4.2 %collective-permute-start.5 = (f32[38,1,128]{2,1,0:T(1,128)S(1)}, f32[38,1,128]{2,1,0:T(1,128)S(1)}, u32[]{:S(2)}, u32[]{:S(2)}) collective-permute-start(f32[38,1,128]{2,1,0:T(1,128)S(1)} %get-tuple-element.11), channel_id=1, source_target_pairs={{0,16},{16,32},{32,48},{48,64},{64,80},{80,96},{96,112},{112,128},... | collective-permute-start | bytes 58376 | tf_op jit(solution)/shard_map/ppermute | solution.py:17
  163.8 0.0 collective-permute-done.4
  163.8 0.9 collective-permute-done.5
  164.6 0.6 fusion.12
  165.2 0.9 reshape.88
  166.1 0.0 all-gather.3.cloned.1.call-update
  166.2 0.0 copy-start.3
  166.2 69.0 %all-gather.3.cloned.1.call-done = bf16[16,38,4096]{2,1,0:T(8,128)(2,1)} async-done(((bf16[1,38,4096]{2,1,0:T(8,128)(2,1)}), bf16[16,38,4096]{2,1,0:T(8,128)(2,1)}) %all-gather.3.cloned.1.call-update) | async-done | bytes 4980752 | tf_op jit(solution)/shard_map/all_gather | solution.py:63
  235.2 5.7 %reshape.89 = bf16[608,4096]{1,0:T(8,128)(2,1)} reshape(bf16[16,38,4096]{2,1,0:T(8,128)(2,1)} %all-gather.3.cloned.1.call-done) | data formatting | bytes 9961472
  240.9 0.0 copy-done.3
  240.9 4.2 %convolution_bitcast_fusion.1 = f32[38,4096]{1,0:T(8,128)} fusion(bf16[608,4096]{1,0:T(8,128)(2,1)} %reshape.89, bf16[38,608]{1,0:T(8,128)(2,1)S(1)} %copy-done.3), kind=kOutput, calls=%fused_computation.2 | convolution fusion | flops 189267968 | bytes 5649536 | tf_op jit(solution)/shard_map/dot_general | solution.py:61
  (6 shorter events, 0.2 us)
Async XLA Ops:
  6.5 1.5 copy-start
  24.4 17.0 %copy-start.1 = (bf16[38,4096]{1,0:T(8,128)(2,1)S(1)}, bf16[38,4096]{1,0:T(8,128)(2,1)}, u32[]{:S(2)}) copy-start(bf16[38,4096]{1,0:T(8,128)(2,1)} %param.13) | copy-start | bytes 933892
  24.4 115.5 %all-to-all-start = ((bf16[32,128,256]{2,1,0:T(8,128)(2,1)}), bf16[32,128,256]{2,1,0:T(8,128)(2,1)S(1)}, u32[]{:S(2)}, u32[]{:S(2)}) async-start(bf16[32,128,256]{2,1,0:T(8,128)(2,1)} %broadcast_select_fusion), calls=%async_computation | async-start | bytes 4194304 | tf_op jit(solution)/shard_map/all_to_all | solution.py:46
  41.2 0.7 copy-start.5
  41.3 98.6 %copy-start.2 = (bf16[3,256,38]{1,2,0:T(8,128)(2,1)S(1)}, bf16[3,256,38]{1,2,0:T(8,128)(2,1)}, u32[]{:S(2)}) copy-start(bf16[3,256,38]{1,2,0:T(8,128)(2,1)} %param.12) | copy-start | bytes 175108
  41.3 193.9 %all-gather.3.cloned.1.call-start = ((), (), s32[]{:S(2)}) async-start(), calls=%async_computation.1 | async-start | bytes 5570560 | tf_op jit(solution)/shard_map/all_gather | solution.py:63
  141.1 7.5 %copy-start.4 = (f32[2,38]{1,0:T(2,128)S(1)}, f32[2,38]{1,0:T(2,128)}, u32[]{:S(2)}) copy-start(f32[2,38]{1,0:T(2,128)} %param.14) | copy-start | bytes 916
  141.6 7.0 %collective-permute-start = (f32[38,1,128]{2,1,0:T(1,128)S(1)}, f32[38,1,128]{2,1,0:T(1,128)S(1)}, u32[]{:S(2)}, u32[]{:S(2)}) collective-permute-start(f32[38,1,128]{2,1,0:T(1,128)S(1)} %get-tuple-element.14), channel_id=1, source_target_pairs={{16,0},{32,16},{48,32},{64,48},{80,64},{96,80},{112,96},{128,112},... | collective-permute-start | bytes 58376 | tf_op jit(solution)/shard_map/ppermute | solution.py:20
  144.3 5.1 %collective-permute-start.1 = (f32[38,1,128]{2,1,0:T(1,128)S(1)}, f32[38,1,128]{2,1,0:T(1,128)S(1)}, u32[]{:S(2)}, u32[]{:S(2)}) collective-permute-start(f32[38,1,128]{2,1,0:T(1,128)S(1)} %get-tuple-element.15), channel_id=1, source_target_pairs={{0,16},{16,32},{32,48},{48,64},{64,80},{80,96},{96,112},{112,128},... | collective-permute-start | bytes 58376 | tf_op jit(solution)/shard_map/ppermute | solution.py:17
  150.0 6.1 %collective-permute-start.2 = (f32[38,1,128]{2,1,0:T(1,128)S(1)}, f32[38,1,128]{2,1,0:T(1,128)S(1)}, u32[]{:S(2)}, u32[]{:S(2)}) collective-permute-start(f32[38,1,128]{2,1,0:T(1,128)S(1)} %get-tuple-element.12), channel_id=1, source_target_pairs={{16,0},{32,16},{48,32},{64,48},{80,64},{96,80},{112,96},{128,112},... | collective-permute-start | bytes 58376 | tf_op jit(solution)/shard_map/ppermute | solution.py:20
  151.9 5.1 %collective-permute-start.3 = (f32[38,1,128]{2,1,0:T(1,128)S(1)}, f32[38,1,128]{2,1,0:T(1,128)S(1)}, u32[]{:S(2)}, u32[]{:S(2)}) collective-permute-start(f32[38,1,128]{2,1,0:T(1,128)S(1)} %get-tuple-element.13), channel_id=1, source_target_pairs={{0,16},{16,32},{32,48},{48,64},{64,80},{80,96},{96,112},{112,128},... | collective-permute-start | bytes 58376 | tf_op jit(solution)/shard_map/ppermute | solution.py:17
  157.6 6.1 %collective-permute-start.4 = (f32[38,1,128]{2,1,0:T(1,128)S(1)}, f32[38,1,128]{2,1,0:T(1,128)S(1)}, u32[]{:S(2)}, u32[]{:S(2)}) collective-permute-start(f32[38,1,128]{2,1,0:T(1,128)S(1)} %get-tuple-element.10), channel_id=1, source_target_pairs={{16,0},{32,16},{48,32},{64,48},{80,64},{96,80},{112,96},{128,112},... | collective-permute-start | bytes 58376 | tf_op jit(solution)/shard_map/ppermute | solution.py:20
  159.5 5.1 %collective-permute-start.5 = (f32[38,1,128]{2,1,0:T(1,128)S(1)}, f32[38,1,128]{2,1,0:T(1,128)S(1)}, u32[]{:S(2)}, u32[]{:S(2)}) collective-permute-start(f32[38,1,128]{2,1,0:T(1,128)S(1)} %get-tuple-element.11), channel_id=1, source_target_pairs={{0,16},{16,32},{32,48},{48,64},{64,80},{80,96},{96,112},{112,128},... | collective-permute-start | bytes 58376 | tf_op jit(solution)/shard_map/ppermute | solution.py:17
  166.2 74.8 %copy-start.3 = (bf16[38,608]{1,0:T(8,128)(2,1)S(1)}, bf16[38,608]{1,0:T(8,128)(2,1)}, u32[]{:S(2)}) copy-start(bf16[38,608]{1,0:T(8,128)(2,1)} %param.15) | copy-start | bytes 138628
Sparse Core Ops, SparseCore 0:
  166.3 68.8 all-gather.2
where the time goes:
time: 253 us; the launch traced here: 252 us
  waiting for transfers between devices  170 us (67%)
  starting transfers between devices  36.2 us (14%)
  local copies, waits for them, and re-layouts  22.4 us (9%)
  between operations  13.6 us (5%)
  other arithmetic  5.22 us (2%)
  matrix products  4.96 us (2%)
    all_to_all x1, waiting for transfers between devices, on_device(): lax.all_to_all(outgoing, 'swath', split_axis=0, concat_axis=0, tiled=True)  97.9 us
    all_gather x1, waiting for transfers between devices, on_device(): lax.all_gather(smoothed, 'chan', axis=0, tiled=True)  69 us
    all_to_all x1, starting transfers between devices, on_device(): lax.all_to_all(outgoing, 'swath', split_axis=0, concat_axis=0, tiled=True)  16.9 us
    gather x1, local copies, waits for them, and re-layouts, on_device(): grid_profiles[slot_rows]  14.6 us
    ppermute x3, starting transfers between devices, extended_2(): lax.ppermute(lax.slice_in_dim(block, block.shape[dim] - width, None, axis...  12.6 us
    unnamed x18, local copies, waits for them, and re-layouts  7.56 us
    ppermute x3, starting transfers between devices, extended_2(): lax.ppermute(lax.slice_in_dim(block, 0, width, axis=dim), axis, backward)  6.62 us
  transfers between devices with their start and end apart: 8, of which 5 were waited for; matrix products, arithmetic and copies ran while one was open for 0% of the time, Pallas kernels for 0%

commit v1 on v0

--- a/solution.py
+++ b/solution.py
@@ -60,7 +60,9 @@
     smoothed = smooth_field.reshape(own_chan, pixel_count).astype(jnp.bfloat16)
     return jnp.dot(
         factor,
-        lax.all_gather(smoothed, "chan", axis=0, tiled=True),
+        jnp.concatenate(
+            lax.all_to_all(jnp.stack([smoothed] * lax.axis_size("chan")), "chan", 0, 0), axis=0
+        ),
         preferred_element_type=jnp.float32,
     )
 

time: 253 us -> 238 us (0.941)
  waiting for transfers between devices: 170 us -> 100 us
  blocking collectives: 0 us -> 67.9 us
  between operations: 13.6 us -> 0.26 us
    all_gather x1 -> x0, waiting for transfers between devices: 69 us -> none  [on_device(): lax.all_gather(smoothed, 'chan', axis=0, tiled=True)]
    all_to_all x0 -> x1, blocking collectives: none -> 67.9 us  [on_device(): lax.all_to_all(jnp.stack([smoothed] * lax.axis_size('chan')), 'chan', 0, 0)]
    unnamed x18, local copies, waits for them, and re-layouts: 7.56 us -> 1.12 us
    reshape x0 -> x1, local copies, waits for them, and re-layouts: none -> 5.75 us  [on_device(): jnp.concatenate(lax.all_to_all(jnp.stack([smoothed] * lax.axis_size('chan...]
  transfers between devices with their start and end apart: 8 -> 7, of which waited for: 5 -> 4; matrix products, arithmetic and copies ran while one was open for 0% -> 0% of each run, Pallas kernels for 0% -> 0%
where the time goes in v1:
time: 238 us; the launch traced here: 237 us
  waiting for transfers between devices  100 us (42%)
  blocking collectives  67.9 us (29%)
  starting transfers between devices  36.1 us (15%)
  local copies, waits for them, and re-layouts  22.4 us (9%)
  other arithmetic  5.24 us (2%)
  matrix products  4.97 us (2%)
    all_to_all x1, waiting for transfers between devices, on_device(): lax.all_to_all(outgoing, 'swath', split_axis=0, concat_axis=0, tiled=True)  97.9 us
    all_to_all x1, blocking collectives, on_device(): lax.all_to_all(jnp.stack([smoothed] * lax.axis_size('chan')), 'chan', 0, 0)  67.9 us
    all_to_all x1, starting transfers between devices, on_device(): lax.all_to_all(outgoing, 'swath', split_axis=0, concat_axis=0, tiled=True)  16.9 us
    gather x1, local copies, waits for them, and re-layouts, on_device(): grid_profiles[slot_rows]  14.6 us
    ppermute x3, starting transfers between devices, extended_2(): lax.ppermute(lax.slice_in_dim(block, block.shape[dim] - width, None, axis...  12.6 us
    ppermute x3, starting transfers between devices, extended_2(): lax.ppermute(lax.slice_in_dim(block, 0, width, axis=dim), axis, backward)  6.62 us
    reshape x1, local copies, waits for them, and re-layouts, on_device(): jnp.concatenate(lax.all_to_all(jnp.stack([smoothed] * lax.axis_size('chan...  5.75 us
  transfers between devices with their start and end apart: 7, of which 4 were waited for; matrix products, arithmetic and copies ran while one was open for 0% of the time, Pallas kernels for 0%

profile of v1, /device:TPU:1, one launch (start us, length us, event | category | flops | bytes accessed | tf_op | source)
XLA Modules:
  0.0 237.3 jit_solution(8014873120014591431)
XLA Ops:
  0.0 0.0 copy-start
  0.0 0.8 iota_compare_fusion
  0.8 0.7 fusion.29
  1.5 0.0 copy-done
  1.5 14.6 %gather_fusion = bf16[4096,256]{1,0:T(8,128)(2,1)S(1)} fusion(bf16[1024,256]{1,0:T(8,128)(2,1)S(1)} %copy-done, s32[4096]{0:T(1024)S(1)} %fusion.29), kind=kCustom, calls=%fused_computation | custom fusion | bytes 4210688 | tf_op jit(solution)/shard_map/gather | solution.py:45
  16.1 1.7 broadcast_select_fusion
  17.8 0.0 copy-start.1
  17.8 16.9 %all-to-all-start = ((bf16[32,128,256]{2,1,0:T(8,128)(2,1)}), bf16[32,128,256]{2,1,0:T(8,128)(2,1)S(1)}, u32[]{:S(2)}, u32[]{:S(2)}) async-start(bf16[32,128,256]{2,1,0:T(8,128)(2,1)} %broadcast_select_fusion), calls=%async_computation | async-start | bytes 4194304 | tf_op jit(solution)/shard_map/all_to_all | solution.py:46
  34.7 0.0 copy-done.1
  34.7 0.0 copy-start.5
  34.8 0.0 copy-start.2
  34.8 0.1 copy.9
  34.9 0.5 copy-done.5
  35.4 97.9 %all-to-all-done = bf16[32,128,256]{2,1,0:T(8,128)(2,1)S(1)} async-done(((bf16[32,128,256]{2,1,0:T(8,128)(2,1)}), bf16[32,128,256]{2,1,0:T(8,128)(2,1)S(1)}, u32[]{:S(2)}, u32[]{:S(2)}) %all-to-all-start) | async-done | bytes 2097184 | tf_op jit(solution)/shard_map/all_to_all | solution.py:46
  133.3 0.0 copy-done.2
  133.3 0.8 convolution_bitcast_fusion
  134.1 0.2 fusion.31
  134.3 0.1 copy.10
  134.4 0.1 copy.12
  134.6 0.0 copy-start.4
  134.6 0.1 copy.11
  134.7 0.3 fusion.14
  135.0 2.8 %collective-permute-start = (f32[38,1,128]{2,1,0:T(1,128)S(1)}, f32[38,1,128]{2,1,0:T(1,128)S(1)}, u32[]{:S(2)}, u32[]{:S(2)}) collective-permute-start(f32[38,1,128]{2,1,0:T(1,128)S(1)} %get-tuple-element.14), channel_id=1, source_target_pairs={{16,0},{32,16},{48,32},{64,48},{80,64},{96,80},{112,96},{128,112},... | collective-permute-start | bytes 58376 | tf_op jit(solution)/shard_map/ppermute | solution.py:20
  137.8 4.2 %collective-permute-start.1 = (f32[38,1,128]{2,1,0:T(1,128)S(1)}, f32[38,1,128]{2,1,0:T(1,128)S(1)}, u32[]{:S(2)}, u32[]{:S(2)}) collective-permute-start(f32[38,1,128]{2,1,0:T(1,128)S(1)} %get-tuple-element.15), channel_id=1, source_target_pairs={{0,16},{16,32},{32,48},{48,64},{64,80},{80,96},{96,112},{112,128},... | collective-permute-start | bytes 58376 | tf_op jit(solution)/shard_map/ppermute | solution.py:17
  142.1 0.0 copy-done.4
  142.1 0.0 collective-permute-done
  142.1 0.8 collective-permute-done.1
  142.9 0.5 fusion.3
  143.5 1.9 collective-permute-start.2
  145.4 4.2 %collective-permute-start.3 = (f32[38,1,128]{2,1,0:T(1,128)S(1)}, f32[38,1,128]{2,1,0:T(1,128)S(1)}, u32[]{:S(2)}, u32[]{:S(2)}) collective-permute-start(f32[38,1,128]{2,1,0:T(1,128)S(1)} %get-tuple-element.13), channel_id=1, source_target_pairs={{0,16},{16,32},{32,48},{48,64},{64,80},{80,96},{96,112},{112,128},... | collective-permute-start | bytes 58376 | tf_op jit(solution)/shard_map/ppermute | solution.py:17
  149.6 0.0 collective-permute-done.2
  149.7 0.9 collective-permute-done.3
  150.5 0.5 fusion.7
  151.1 1.9 collective-permute-start.4
  153.0 4.2 %collective-permute-start.5 = (f32[38,1,128]{2,1,0:T(1,128)S(1)}, f32[38,1,128]{2,1,0:T(1,128)S(1)}, u32[]{:S(2)}, u32[]{:S(2)}) collective-permute-start(f32[38,1,128]{2,1,0:T(1,128)S(1)} %get-tuple-element.11), channel_id=1, source_target_pairs={{0,16},{16,32},{32,48},{48,64},{64,80},{80,96},{96,112},{112,128},... | collective-permute-start | bytes 58376 | tf_op jit(solution)/shard_map/ppermute | solution.py:17
  157.2 0.0 collective-permute-done.4
  157.2 0.9 collective-permute-done.5
  158.1 0.6 fusion.12
  158.7 0.1 copy.13
  158.9 0.6 stack.2
  159.5 67.9 %all_to_all.10 = bf16[16,38,4096]{2,1,0:T(8,128)(2,1)} all-to-all(bf16[16,38,4096]{2,1,0:T(8,128)(2,1)S(1)} %stack.2), channel_id=1, replica_groups=mesh['swath'=32,'chan'=16] {'chan'}, dimensions={0} | all-to-all | bytes 9961472 | tf_op jit(solution)/shard_map/all_to_all | solution.py:64
  227.4 0.0 copy-start.3
  227.4 5.7 %reshape.83 = bf16[608,4096]{1,0:T(8,128)(2,1)} reshape(bf16[16,38,4096]{2,1,0:T(8,128)(2,1)} %all_to_all.10) | data formatting | bytes 9961472 | tf_op jit(solution)/shard_map/reshape | solution.py:63
  233.1 0.0 copy-done.3
  233.1 4.2 %convolution_bitcast_fusion.1 = f32[38,4096]{1,0:T(8,128)} fusion(bf16[608,4096]{1,0:T(8,128)(2,1)} %reshape.83, bf16[38,608]{1,0:T(8,128)(2,1)S(1)} %copy-done.3), kind=kOutput, calls=%fused_computation.2 | convolution fusion | flops 189267968 | bytes 5649536 | tf_op jit(solution)/shard_map/dot_general | solution.py:61
  (7 shorter events, 0.2 us)
Async XLA Ops:
  0.0 1.5 copy-start
  17.8 16.9 %copy-start.1 = (bf16[38,4096]{1,0:T(8,128)(2,1)S(1)}, bf16[38,4096]{1,0:T(8,128)(2,1)}, u32[]{:S(2)}) copy-start(bf16[38,4096]{1,0:T(8,128)(2,1)} %param.13) | copy-start | bytes 933892
  17.8 115.5 %all-to-all-start = ((bf16[32,128,256]{2,1,0:T(8,128)(2,1)}), bf16[32,128,256]{2,1,0:T(8,128)(2,1)S(1)}, u32[]{:S(2)}, u32[]{:S(2)}) async-start(bf16[32,128,256]{2,1,0:T(8,128)(2,1)} %broadcast_select_fusion), calls=%async_computation | async-start | bytes 4194304 | tf_op jit(solution)/shard_map/all_to_all | solution.py:46
  34.7 0.7 copy-start.5
  34.8 98.6 %copy-start.2 = (bf16[3,256,38]{1,2,0:T(8,128)(2,1)S(1)}, bf16[3,256,38]{1,2,0:T(8,128)(2,1)}, u32[]{:S(2)}) copy-start(bf16[3,256,38]{1,2,0:T(8,128)(2,1)} %param.12) | copy-start | bytes 175108
  134.6 7.5 %copy-start.4 = (f32[2,38]{1,0:T(2,128)S(1)}, f32[2,38]{1,0:T(2,128)}, u32[]{:S(2)}) copy-start(f32[2,38]{1,0:T(2,128)} %param.14) | copy-start | bytes 916
  135.0 7.0 %collective-permute-start = (f32[38,1,128]{2,1,0:T(1,128)S(1)}, f32[38,1,128]{2,1,0:T(1,128)S(1)}, u32[]{:S(2)}, u32[]{:S(2)}) collective-permute-start(f32[38,1,128]{2,1,0:T(1,128)S(1)} %get-tuple-element.14), channel_id=1, source_target_pairs={{16,0},{32,16},{48,32},{64,48},{80,64},{96,80},{112,96},{128,112},... | collective-permute-start | bytes 58376 | tf_op jit(solution)/shard_map/ppermute | solution.py:20
  137.8 5.1 %collective-permute-start.1 = (f32[38,1,128]{2,1,0:T(1,128)S(1)}, f32[38,1,128]{2,1,0:T(1,128)S(1)}, u32[]{:S(2)}, u32[]{:S(2)}) collective-permute-start(f32[38,1,128]{2,1,0:T(1,128)S(1)} %get-tuple-element.15), channel_id=1, source_target_pairs={{0,16},{16,32},{32,48},{48,64},{64,80},{80,96},{96,112},{112,128},... | collective-permute-start | bytes 58376 | tf_op jit(solution)/shard_map/ppermute | solution.py:17
  143.5 6.1 %collective-permute-start.2 = (f32[38,1,128]{2,1,0:T(1,128)S(1)}, f32[38,1,128]{2,1,0:T(1,128)S(1)}, u32[]{:S(2)}, u32[]{:S(2)}) collective-permute-start(f32[38,1,128]{2,1,0:T(1,128)S(1)} %get-tuple-element.12), channel_id=1, source_target_pairs={{16,0},{32,16},{48,32},{64,48},{80,64},{96,80},{112,96},{128,112},... | collective-permute-start | bytes 58376 | tf_op jit(solution)/shard_map/ppermute | solution.py:20
  145.4 5.1 %collective-permute-start.3 = (f32[38,1,128]{2,1,0:T(1,128)S(1)}, f32[38,1,128]{2,1,0:T(1,128)S(1)}, u32[]{:S(2)}, u32[]{:S(2)}) collective-permute-start(f32[38,1,128]{2,1,0:T(1,128)S(1)} %get-tuple-element.13), channel_id=1, source_target_pairs={{0,16},{16,32},{32,48},{48,64},{64,80},{80,96},{96,112},{112,128},... | collective-permute-start | bytes 58376 | tf_op jit(solution)/shard_map/ppermute | solution.py:17
  151.1 6.1 %collective-permute-start.4 = (f32[38,1,128]{2,1,0:T(1,128)S(1)}, f32[38,1,128]{2,1,0:T(1,128)S(1)}, u32[]{:S(2)}, u32[]{:S(2)}) collective-permute-start(f32[38,1,128]{2,1,0:T(1,128)S(1)} %get-tuple-element.10), channel_id=1, source_target_pairs={{16,0},{32,16},{48,32},{64,48},{80,64},{96,80},{112,96},{128,112},... | collective-permute-start | bytes 58376 | tf_op jit(solution)/shard_map/ppermute | solution.py:20
  153.0 5.1 %collective-permute-start.5 = (f32[38,1,128]{2,1,0:T(1,128)S(1)}, f32[38,1,128]{2,1,0:T(1,128)S(1)}, u32[]{:S(2)}, u32[]{:S(2)}) collective-permute-start(f32[38,1,128]{2,1,0:T(1,128)S(1)} %get-tuple-element.11), channel_id=1, source_target_pairs={{0,16},{16,32},{32,48},{48,64},{64,80},{80,96},{96,112},{112,128},... | collective-permute-start | bytes 58376 | tf_op jit(solution)/shard_map/ppermute | solution.py:17
  227.4 5.8 %copy-start.3 = (bf16[38,608]{1,0:T(8,128)(2,1)S(1)}, bf16[38,608]{1,0:T(8,128)(2,1)}, u32[]{:S(2)}) copy-start(bf16[38,608]{1,0:T(8,128)(2,1)} %param.15) | copy-start | bytes 138628
